TPU v7x, 256 devices: a whole 4x4x8 slice. The times are simulated.
256 devices in a mesh: seq: 16 (over y, x), chan: 16 (over z, core).
Axes of the slice: x: 4, y: 4, z: 8, core: 2. Of those that a mesh axis runs over, the one named last changes fastest.
Arguments:
- tokens: bfloat16 [57344, 2048], P('seq', 'chan'), may hold values from -6 to 6
- w_query: bfloat16 [2048, 256], replicated, may hold values from -0.125 to 0.125
- w_key: bfloat16 [2048, 256], replicated, may hold values from -0.125 to 0.125
- w_value: bfloat16 [2048, 2048], P(None, 'chan'), may hold values from -0.125 to 0.125
- w_out: bfloat16 [2048, 2048], replicated, may hold values from -0.125 to 0.125
- gain: float32 [2048], replicated, may hold values from 0.1 to 1.9
Outputs:
- mixed: bfloat16 [57344, 2048], P('seq', 'chan')
All inputs are finite; a program needn't handle non-finite values.
Results may differ from a plain program's by a relative error of at most 0.019.
Values may be sent and summed in bfloat16 or wider, within the bound.
A program may use at most 128 MiB of HBM per device.

v0:
```python
import jax
import jax.numpy as jnp
from jax import lax
from jax.sharding import PartitionSpec as P

HEADS = 16
FEAT = 16
HEAD_DIM = 128
BLOCK = 896


def feature_parts(rows):
    linear = rows * FEAT ** (-0.25)
    square = (rows[..., :, None] * rows[..., None, :]).reshape(rows.shape[:-1] + (FEAT * FEAT,)) * (
        2.0 * FEAT
    ) ** (-0.5)
    return (linear, square)


def per_device(tokens, w_query, w_key, w_value, w_out, gain):
    highest = lax.Precision.HIGHEST
    groups = lax.axis_size("chan")
    per_group = HEADS // groups
    my_group = lax.axis_index("chan")
    my_slab = lax.axis_index("seq")
    tok_rows = tokens.shape[0]
    query_cols = per_group * FEAT
    value_cols = per_group * HEAD_DIM
    query_mine = lax.dynamic_slice_in_dim(w_query, my_group * query_cols, query_cols, 1)
    key_mine = lax.dynamic_slice_in_dim(w_key, my_group * query_cols, query_cols, 1)
    initial = (
        jnp.zeros((tok_rows, query_cols), jnp.float32),
        jnp.zeros((tok_rows, query_cols), jnp.float32),
        jnp.zeros((tok_rows, value_cols), jnp.float32),
    )
    piece = lax.all_gather(tokens, "chan", axis=1, tiled=True)
    query_sum, key_sum, value_sum = tuple(
        (
            jnp.dot(piece, weight, preferred_element_type=jnp.float32)
            for weight in (query_mine, key_mine, w_value)
        )
    )
    query_rows = query_sum.astype(jnp.bfloat16)
    key_rows = key_sum.astype(jnp.bfloat16)
    value_rows = value_sum.astype(jnp.bfloat16)
    blocks = tok_rows // BLOCK
    query_blocks = query_rows.reshape(blocks, BLOCK, per_group, FEAT)
    key_blocks = key_rows.reshape(blocks, BLOCK, per_group, FEAT)
    value_blocks = value_rows.reshape(blocks, BLOCK, per_group, HEAD_DIM)
    value_f32 = value_blocks.astype(jnp.float32)
    key_linear, key_square = feature_parts(key_blocks.astype(jnp.float32))
    own_zero = jnp.sum(value_f32, axis=1)
    own_one = jnp.einsum("bthf,bthe->bhfe", key_linear, value_f32, precision=highest)
    own_two = jnp.einsum("bthf,bthe->bhfe", key_square, value_f32, precision=highest)
    own = (own_zero, own_one, own_two)
    slab_total = tuple((jnp.sum(member, axis=0) for member in own))
    initial = tuple((jnp.zeros_like(member) for member in slab_total))
    pieces = (
        lax.all_gather(slab_total[0][None].astype(jnp.bfloat16), "seq", axis=0, tiled=True).astype(
            jnp.float32
        ),
        lax.all_gather(slab_total[1][None].astype(jnp.bfloat16), "seq", axis=0, tiled=True).astype(
            jnp.float32
        ),
        lax.all_gather(slab_total[2][None].astype(jnp.bfloat16), "seq", axis=0, tiled=True).astype(
            jnp.float32
        ),
    )
    count = pieces[0].shape[0]
    order = jnp.arange(count, dtype=jnp.int32)
    earlier_mask = order < my_slab
    prefix = tuple(
        (
            total
            + jnp.sum(
                jnp.where(earlier_mask.reshape((count,) + (1,) * (piece.ndim - 1)), piece, 0.0),
                axis=0,
            )
            for total, piece in zip(initial, pieces)
        )
    )
    earlier = tuple(
        (
            jnp.concatenate([jnp.zeros_like(member[:1]), jnp.cumsum(member, axis=0)[:-1]], axis=0)
            + base[None]
            for member, base in zip(own, prefix)
        )
    )
    query_linear, query_square = feature_parts(query_blocks.astype(jnp.float32))
    inter = earlier[0][:, None] + jnp.einsum(
        "bthf,bhfe->bthe", query_linear, earlier[1], precision=highest
    )
    inter = inter + jnp.einsum("bthf,bhfe->bthe", query_square, earlier[2], precision=highest)
    scores = jnp.einsum(
        "bthf,bshf->bhts", query_blocks, key_blocks, preferred_element_type=jnp.float32
    ) * FEAT ** (-0.5)
    kernel = 1.0 + scores + 0.5 * scores * scores
    causal = jnp.arange(BLOCK)[:, None] >= jnp.arange(BLOCK)[None, :]
    weights = jnp.where(causal, kernel, 0.0).astype(jnp.bfloat16)
    intra = jnp.einsum("bhts,bshe->bthe", weights, value_blocks, preferred_element_type=jnp.float32)
    numerator = (intra + inter).reshape(tok_rows, per_group, HEAD_DIM)
    gain_mine = lax.dynamic_slice_in_dim(gain, my_group * value_cols, value_cols, 0).reshape(
        per_group, HEAD_DIM
    )
    mean_square = jnp.mean(numerator * numerator, axis=-1, keepdims=True)
    hidden = (
        (numerator * lax.rsqrt(mean_square + 1e-05) * gain_mine)
        .astype(jnp.bfloat16)
        .reshape(tok_rows, value_cols)
    )
    out_mine = lax.dynamic_slice_in_dim(w_out, my_group * value_cols, value_cols, 0)
    partial_value = jnp.dot(hidden, out_mine, preferred_element_type=jnp.float32)
    partial_value = lax.optimization_barrier(partial_value.astype(jnp.bfloat16)).astype(jnp.float32)
    mixed = lax.psum_scatter(
        partial_value.astype(jnp.bfloat16), "chan", scatter_dimension=1, tiled=True
    )
    return mixed


def solution(mesh):
    return jax.shard_map(
        per_device,
        mesh=mesh,
        in_specs=(P("seq", "chan"), P(), P(), P(None, "chan"), P(), P()),
        out_specs=P("seq", "chan"),
        check_vma=False,
    )
```

profile of v0, /device:TPU:2, one launch (start us, length us, event | category | flops | bytes accessed | tf_op | source)
XLA Modules:
  0.0 357.5 jit_solution(1797674125439511556)
XLA Ops:
  6.5 0.0 copy-start
  6.5 0.0 all-gather.7.cloned.1.call-start
  6.5 0.7 all-gather.7.cloned.1.call-update
  7.3 0.0 all-gather.9.cloned.1.call-start
  7.3 0.8 dynamic_slice.14
  8.1 0.2 iota_compare_fusion
  8.3 96.7 %all-gather.7.cloned.1.call-done = bf16[3584,2048]{1,0:T(8,128)(2,1)} async-done(((bf16[3584,128]{1,0:T(8,128)(2,1)}), bf16[3584,2048]{1,0:T(8,128)(2,1)}) %all-gather.7.cloned.1.call-update) | async-done | bytes 14680080 | tf_op jit(solution)/shard_map/all_gather | solution.py:36
  105.0 9.2 %fusion.51 = (bf16[128]{0:T(256)(128)(2,1)S(1)}, bf16[3584,128]{1,0:T(8,128)(2,1)S(1)}) fusion(bf16[3584,2048]{1,0:T(8,128)(2,1)} %all-gather.7.cloned.1.call-done, bf16[2048,128]{1,0:T(8,128)(2,1)} %param.9), kind=kOutput, calls=%fused_computation.68 | convolution fusion | flops 1879965568 | bytes 16122112 | tf_op jit(solution)/shard_map/dot_general | solution.py:39
  114.3 0.1 convert_reduce_fusion
  114.4 0.0 copy-done
  114.4 9.4 %convolution_convert_fusion.2 = bf16[16,3584]{1,0:T(8,128)(2,1)S(1)} fusion(bf16[3584,2048]{1,0:T(8,128)(2,1)} %all-gather.7.cloned.1.call-done, bf16[2048,256]{1,0:T(8,128)(2,1)S(1)} %copy-done, s32[]{:T(128)S(6)} %select_n.25), kind=kOutput, calls=%fused_computation.3 | convolution fusion | flops 234938368 | bytes 15319044 | tf_op jit(solution)/shard_map/dot_general | solution.py:39
  123.8 0.5 fusion.50
  124.4 20.3 %all-gather.3 = bf16[16,1,128]{2,1,0:T(2,128)(2,1)S(1)} all-gather(bf16[1,1,128]{2,1,0:T(2,128)(2,1)S(1)} %bitcast.100), channel_id=2, replica_groups=mesh['seq'=16,'chan'=16] {'seq'}, dimensions={0}, use_global_device_ids=true | all-gather | bytes 4352 | tf_op jit(solution)/shard_map/all_gather | solution.py:59
  144.7 0.1 fusion.32
  144.8 0.0 copy-start.3
  144.8 21.4 %all-gather.1 = bf16[256,128]{1,0:T(8,128)(2,1)S(1)} all-gather(bf16[16,128]{1,0:T(8,128)(2,1)S(1)} %get-tuple-element.7), channel_id=3, replica_groups=mesh['seq'=16,'chan'=16] {'seq'}, dimensions={0}, use_global_device_ids=true | all-gather | bytes 69632 | tf_op jit(solution)/shard_map/all_gather | solution.py:62
  166.2 0.4 multiply_multiply_fusion.1
  166.6 2.5 fusion.49
  169.0 0.0 copy-done.3
  169.0 0.0 all-gather.9.cloned.1.call-update
  169.1 0.0 reduce-scatter.4.cloned.1.call-start
  169.1 0.4 fusion.8
  169.5 0.0 copy-start.2
  169.6 0.1 fusion.20
  169.7 0.1 fusion.37
  169.8 0.0 slice-start.1
  169.8 9.6 %convolution_convert_fusion.3 = bf16[16,3584]{1,0:T(8,128)(2,1)S(1)} fusion(bf16[3584,2048]{1,0:T(8,128)(2,1)} %all-gather.7.cloned.1.call-done, bf16[2048,256]{1,0:T(8,128)(2,1)} %param.7, s32[]{:T(128)S(6)} %select_n.25), kind=kOutput, calls=%fused_computation.4 | convolution fusion | flops 234938368 | bytes 15319044 | tf_op jit(solution)/shard_map/dot_general | solution.py:39
  179.4 0.0 copy-done.2
  179.4 0.0 slice-done.1
  179.4 0.0 slice-start
  179.4 2.9 fusion.16
  182.3 2.2 multiply_multiply_fusion
  184.5 29.4 %all-gather.9.cloned.1.call-done = bf16[4096,128]{1,0:T(8,128)(2,1)} async-done(((bf16[256,128]{1,0:T(8,128)(2,1)}), bf16[4096,128]{1,0:T(8,128)(2,1)}) %all-gather.9.cloned.1.call-update) | async-done | bytes 1048592 | tf_op jit(solution)/shard_map/all_gather | solution.py:65
  213.9 1.5 fusion
  215.4 0.0 slice-done
  215.4 5.6 %fusion.6 = f32[4,128,896]{2,1,0:T(8,128)} fusion(f32[4,896,256]{1,2,0:T(8,128)} %bitcast.84, f32[3,1,256,128]{3,2,0,1:T(8,128)S(1)} %slice-done, f32[256,128]{1,0:T(8,128)S(1)} %fusion), kind=kOutput, calls=%fused_computation.20 | convolution fusion | flops 1409417216 | bytes 6029312 | tf_op jit(solution)/shard_map/bthf,bhfe->bthe/dot_general | solution.py:93
  221.0 8.5 %multiply_reduce_fusion = (f32[4,896]{1,0:T(4,128)S(1)}, f32[4,896,1,128]{1,3,0,2:T(8,128)}) fusion(f32[4,128,896]{2,1,0:T(8,128)} %fusion.6, f32[4,128,896]{2,1,0:T(8,128)} %fusion.16, f32[4,128]{1,0:T(4,128)S(1)} %add_bitcast_fusion, bf16[4,896,128]{2,1,0:T(8,128)(2,1)S(1)} %bitcast.88, pred[896,896]{1,0:T(8,128)(4,1)S(1)} %iota_compare_fusion, ...), kind=kOutput, calls=%fused_computation.18 | convolution fusion | flops 949613056 | bytes 7471104 | tf_op jit(solution)/shard_map/bhts,bshe->bthe/dot_general | solution.py:100
  229.5 1.8 copy.41
  231.3 0.5 fusion.3
  231.9 8.3 %convolution_convert_fusion = bf16[3584,2048]{1,0:T(8,128)(2,1)} fusion(bf16[3584,128]{1,0:T(8,128)(2,1)S(1)} %fusion.3, bf16[2048,2048]{1,0:T(8,128)(2,1)} %param.10, s32[]{:T(128)S(6)} %select_n.30), kind=kOutput, calls=%fused_computation | convolution fusion | flops 1886388224 | bytes 16121860 | tf_op jit(solution)/shard_map/dot_general | solution.py:112
  240.2 18.8 %copy.45 = bf16[3584,2048]{0,1:T(8,128)(2,1)} copy(bf16[3584,2048]{1,0:T(8,128)(2,1)} %convolution_convert_fusion) | data formatting | bytes 29360128
  259.0 0.0 reduce-scatter.4.cloned.1.call-update
  259.0 0.0 copy-start.1
  259.0 89.8 %reduce-scatter.4.cloned.1.call-done = bf16[128,3584]{1,0:T(8,128)(2,1)} async-done(((bf16[2048,3584]{1,0:T(8,128)(2,1)}), bf16[128,3584]{1,0:T(8,128)(2,1)}) %reduce-scatter.4.cloned.1.call-update) | async-done | bytes 917520
  348.8 2.2 copy.46
  351.0 0.0 copy-done.1
  (7 shorter events, 0.1 us)
Async XLA Ops:
  6.5 107.9 %copy-start = (bf16[2048,256]{1,0:T(8,128)(2,1)S(1)}, bf16[2048,256]{1,0:T(8,128)(2,1)}, u32[]{:S(2)}) copy-start(bf16[2048,256]{1,0:T(8,128)(2,1)} %param.8) | copy-start | bytes 3145732
  6.5 98.5 %all-gather.7.cloned.1.call-start = ((), (), s32[]{:S(2)}) async-start(), calls=%async_computation.1 | async-start | bytes 15597568 | tf_op jit(solution)/shard_map/all_gather | solution.py:36
  7.3 206.7 %all-gather.9.cloned.1.call-start = ((), (), s32[]{:S(2)}) async-start(), calls=%async_computation.2 | async-start | bytes 1114112 | tf_op jit(solution)/shard_map/all_gather | solution.py:65
  144.8 24.3 %copy-start.3 = (f32[4,1,16,128]{3,2,0,1:T(8,128)}, f32[4,1,16,128]{3,2,0,1:T(8,128)S(1)}, u32[]{:S(2)}) copy-start(f32[4,1,16,128]{3,2,0,1:T(8,128)S(1)} %fusion.32) | copy-start | bytes 98308
  169.1 179.7 %reduce-scatter.4.cloned.1.call-start = ((), (), s32[]{:S(2)}) async-start(), calls=%async_computation.3 | async-start | bytes 15597568
  169.5 9.9 %copy-start.2 = (f32[4,1,256,128]{3,2,0,1:T(8,128)}, f32[4,1,256,128]{3,2,0,1:T(8,128)S(1)}, u32[]{:S(2)}) copy-start(f32[4,1,256,128]{3,2,0,1:T(8,128)S(1)} %fusion.8) | copy-start | bytes 1572868
  169.8 9.6 %slice-start.1 = ((f32[4,1,16,128]{3,2,0,1:T(8,128)}), f32[3,1,16,128]{3,2,0,1:T(8,128)S(1)}, s32[]{:S(2)}) async-start(f32[4,1,16,128]{3,2,0,1:T(8,128)} %copy-done.3), calls=%async_computation.5 | async-start | bytes 49152 | tf_op jit(solution)/shard_map/slice | solution.py:84
  179.4 36.0 %slice-start = ((f32[4,1,256,128]{3,2,0,1:T(8,128)}), f32[3,1,256,128]{3,2,0,1:T(8,128)S(1)}, s32[]{:S(2)}) async-start(f32[4,1,256,128]{3,2,0,1:T(8,128)} %copy-done.2), calls=%async_computation.4 | async-start | bytes 786432 | tf_op jit(solution)/shard_map/slice | solution.py:84
  259.0 92.0 %copy-start.1 = (bf16[2048,256]{1,0:T(8,128)(2,1)S(1)}, bf16[2048,256]{1,0:T(8,128)(2,1)}, u32[]{:S(2)}) copy-start(bf16[2048,256]{1,0:T(8,128)(2,1)} %param.8) | copy-start | bytes 3145732
Sparse Core Ops, SparseCore 0:
  9.1 95.8 all-gather.6
  169.2 44.6 all-gather.8
  259.1 89.6 reduce-scatter.3
where the time goes:
time: 358 us
  waiting for transfers between devices  217 us (61%)
  matrix products  56.4 us (16%)
  blocking collectives  41.7 us (12%)
  local copies, waits for them, and re-layouts  23.6 us (7%)
  between operations  13.3 us (4%)
  other arithmetic  5.75 us (2%)
    all_gather x1, waiting for transfers between devices, per_device(): piece = lax.all_gather(tokens, 'chan', axis=1, tiled=True)  96.7 us
    unnamed x4, waiting for transfers between devices  90.5 us
    all_gather x1, waiting for transfers between devices, per_device(): lax.all_gather(slab_total[2][None].astype(jnp.bfloat16), 'seq', axis=0, t...  29.4 us
    dot_general x3, matrix products, per_device(): jnp.dot(piece, weight, preferred_element_type=jnp.float32)  28.2 us
    all_gather x1, blocking collectives, per_device(): lax.all_gather(slab_total[1][None].astype(jnp.bfloat16), 'seq', axis=0, t...  21.4 us
    unnamed x10, local copies, waits for them, and re-layouts  21 us
    all_gather x1, blocking collectives, per_device(): lax.all_gather(slab_total[0][None].astype(jnp.bfloat16), 'seq', axis=0, t...  20.3 us
    dot_general x1, matrix products, per_device(): jnp.einsum('bhts,bshe->bthe', weights, value_blocks, preferred_element_ty...  8.45 us
  transfers between devices with their start and end apart: 3, of which 3 were waited for; matrix products, arithmetic and copies ran while one was open for 5% of the time, Pallas kernels for 0%

commit v1 on v0

--- a/solution.py
+++ b/solution.py
@@ -7,6 +7,13 @@
 FEAT = 16
 HEAD_DIM = 128
 BLOCK = 896
+
+
+def all_by_exchange(array, axis, along):
+    size = lax.axis_size(axis)
+    blocks = jnp.stack([array for _ in range(size)])
+    blocks = lax.all_to_all(blocks, axis, split_axis=0, concat_axis=0)
+    return jnp.concatenate(blocks, axis=along)
 
 
 def feature_parts(rows):
@@ -62,9 +69,7 @@
         lax.all_gather(slab_total[1][None].astype(jnp.bfloat16), "seq", axis=0, tiled=True).astype(
             jnp.float32
         ),
-        lax.all_gather(slab_total[2][None].astype(jnp.bfloat16), "seq", axis=0, tiled=True).astype(
-            jnp.float32
-        ),
+        all_by_exchange(slab_total[2][None].astype(jnp.bfloat16), "seq", 0).astype(jnp.float32),
     )
     count = pieces[0].shape[0]
     order = jnp.arange(count, dtype=jnp.int32)

time: 358 us -> 336 us (0.939)
  waiting for transfers between devices: 217 us -> 184 us
  starting transfers between devices: 0.08 us -> 6.19 us
    all_gather x1 -> x0, waiting for transfers between devices: 29.4 us -> none  [per_device(): lax.all_gather(slab_total[2][None].astype(jnp.bfloat16), 'seq', axis=0, t...]
    all_to_all x0 -> x1, starting transfers between devices: none -> 5.97 us  [all_by_exchange(): blocks = lax.all_to_all(blocks, axis, split_axis=0, concat_axis=0)]
    unnamed x4 -> x3, waiting for transfers between devices: 90.5 us -> 87.9 us
    unnamed x10 -> x22, local copies, waits for them, and re-layouts: 21 us -> 21 us
  transfers between devices with their start and end apart: 3 -> 3, of which waited for: 3 -> 2; matrix products, arithmetic and copies ran while one was open for 5% -> 5% of each run, Pallas kernels for 0% -> 0%
where the time goes in v1:
time: 336 us; the launch traced here: 335 us
  waiting for transfers between devices  184 us (55%)
  matrix products  56.2 us (17%)
  blocking collectives  43.6 us (13%)
  local copies, waits for them, and re-layouts  25.5 us (8%)
  between operations  13.6 us (4%)
  starting transfers between devices  6.19 us (2%)
  other arithmetic  5.5 us (2%)
    all_gather x1, waiting for transfers between devices, per_device(): piece = lax.all_gather(tokens, 'chan', axis=1, tiled=True)  96.3 us
    unnamed x3, waiting for transfers between devices  87.9 us
    dot_general x3, matrix products, per_device(): jnp.dot(piece, weight, preferred_element_type=jnp.float32)  28.2 us
    all_gather x1, blocking collectives, per_device(): lax.all_gather(slab_total[1][None].astype(jnp.bfloat16), 'seq', axis=0, t...  23.3 us
    unnamed x22, local copies, waits for them, and re-layouts  21 us
    all_gather x1, blocking collectives, per_device(): lax.all_gather(slab_total[0][None].astype(jnp.bfloat16), 'seq', axis=0, t...  20.3 us
    dot_general x1, matrix products, per_device(): jnp.dot(hidden, out_mine, preferred_element_type=jnp.float32)  8.32 us
    dot_general x1, matrix products, per_device(): jnp.einsum('bhts,bshe->bthe', weights, value_blocks, preferred_element_ty...  8.24 us
  transfers between devices with their start and end apart: 3, of which 2 were waited for; matrix products, arithmetic and copies ran while one was open for 5% of the time, Pallas kernels for 0%

profile of v1, /device:TPU:2, one launch (start us, length us, event | category | flops | bytes accessed | tf_op | source)
XLA Modules:
  0.0 334.7 jit_solution(1636277537946885014)
XLA Ops:
  6.5 0.0 copy-start
  6.5 0.0 all-gather.5.cloned.1.call-start
  6.5 0.7 all-gather.5.cloned.1.call-update
  7.3 1.2 dynamic_slice.14
  8.5 0.0 copy-start.5
  8.5 0.2 iota_compare_fusion
  8.8 96.3 %all-gather.5.cloned.1.call-done = bf16[3584,2048]{1,0:T(8,128)(2,1)} async-done(((bf16[3584,128]{1,0:T(8,128)(2,1)}), bf16[3584,2048]{1,0:T(8,128)(2,1)}) %all-gather.5.cloned.1.call-update) | async-done | bytes 14680080 | tf_op jit(solution)/shard_map/all_gather | solution.py:43
  105.0 9.2 %fusion.51 = (bf16[128]{0:T(256)(128)(2,1)S(1)}, bf16[3584,128]{1,0:T(8,128)(2,1)S(1)}) fusion(bf16[3584,2048]{1,0:T(8,128)(2,1)} %all-gather.5.cloned.1.call-done, bf16[2048,128]{1,0:T(8,128)(2,1)} %param.9), kind=kOutput, calls=%fused_computation.68 | convolution fusion | flops 1879965568 | bytes 16122112 | tf_op jit(solution)/shard_map/dot_general | solution.py:46
  114.3 0.1 convert_reduce_fusion
  114.4 0.0 copy-done
  114.4 9.4 %convolution_convert_fusion.2 = bf16[16,3584]{1,0:T(8,128)(2,1)S(1)} fusion(bf16[3584,2048]{1,0:T(8,128)(2,1)} %all-gather.5.cloned.1.call-done, bf16[2048,256]{1,0:T(8,128)(2,1)S(1)} %copy-done, s32[]{:T(128)S(6)} %select_n.33), kind=kOutput, calls=%fused_computation.3 | convolution fusion | flops 234938368 | bytes 15319044 | tf_op jit(solution)/shard_map/dot_general | solution.py:46
  123.8 1.1 fusion.50
  125.0 20.3 %all-gather.2 = bf16[16,1,128]{2,1,0:T(2,128)(2,1)S(1)} all-gather(bf16[1,1,128]{2,1,0:T(2,128)(2,1)S(1)} %bitcast.100), channel_id=2, replica_groups=mesh['seq'=16,'chan'=16] {'seq'}, dimensions={0}, use_global_device_ids=true | all-gather | bytes 4352 | tf_op jit(solution)/shard_map/all_gather | solution.py:66
  145.3 0.1 fusion.32
  145.4 0.4 multiply_multiply_fusion.1
  145.7 1.8 fusion.49
  147.6 0.2 fusion.8
  147.8 0.0 copy-start.2
  147.8 1.2 stack.2
  149.0 6.0 %all-to-all-start = ((bf16[16,1,1,256,128]{4,3,2,1,0:T(8,128)(2,1)}), bf16[16,1,1,256,128]{4,3,2,1,0:T(8,128)(2,1)S(1)}, u32[]{:S(2)}, u32[]{:S(2)}) async-start(bf16[16,1,1,256,128]{4,3,2,1,0:T(8,128)(2,1)} %stack.2), calls=%async_computation | async-start | bytes 2097152 | tf_op jit(solution)/shard_map/all_to_all | solution.py:15
  155.0 0.2 reduce-scatter.4.cloned.1.call-start
  155.2 0.6 reduce_window_sum.33
  155.8 0.0 copy-done.5
  155.8 0.1 fusion.37
  155.9 0.0 copy-start.4
  155.9 0.0 copy-start.3
  155.9 0.0 copy-start.6
  155.9 9.6 %convolution_convert_fusion.3 = bf16[16,3584]{1,0:T(8,128)(2,1)S(1)} fusion(bf16[3584,2048]{1,0:T(8,128)(2,1)} %all-gather.5.cloned.1.call-done, bf16[2048,256]{1,0:T(8,128)(2,1)} %param.7, s32[]{:T(128)S(6)} %select_n.33), kind=kOutput, calls=%fused_computation.4 | convolution fusion | flops 234938368 | bytes 15319044 | tf_op jit(solution)/shard_map/dot_general | solution.py:46
  165.5 0.0 copy-done.4
  165.5 0.6 add_bitcast_fusion
  166.1 0.0 copy-done.2
  166.2 0.0 copy-start.7
  166.2 0.0 copy-done.3
  166.2 23.3 %all-gather.1 = bf16[256,128]{1,0:T(8,128)(2,1)S(1)} all-gather(bf16[16,128]{1,0:T(8,128)(2,1)S(1)} %copy-done.3), channel_id=3, replica_groups=mesh['seq'=16,'chan'=16] {'seq'}, dimensions={0}, use_global_device_ids=true | all-gather | bytes 69632 | tf_op jit(solution)/shard_map/all_gather | solution.py:69
  189.4 0.0 copy-done.6
  189.4 0.1 fusion.20
  189.5 0.0 slice-start
  189.5 2.9 fusion.16
  192.4 2.2 multiply_multiply_fusion
  194.6 0.0 copy-start.8
  194.6 0.0 all-to-all-done
  194.6 0.0 copy-done.7
  194.6 0.3 fusion
  194.9 0.0 slice-done
  194.9 5.6 %fusion.6 = f32[4,128,896]{2,1,0:T(8,128)} fusion(f32[4,896,256]{1,2,0:T(8,128)} %bitcast.85, f32[3,1,256,128]{3,2,0,1:T(8,128)S(1)} %slice-done, f32[256,128]{1,0:T(8,128)S(1)} %fusion), kind=kOutput, calls=%fused_computation.20 | convolution fusion | flops 1409417216 | bytes 6029312 | tf_op jit(solution)/shard_map/bthf,bhfe->bthe/dot_general | solution.py:98
  200.5 0.0 copy-done.8
  200.5 8.2 %multiply_reduce_fusion = (f32[4,896]{1,0:T(4,128)S(1)}, f32[4,896,1,128]{1,3,0,2:T(8,128)}) fusion(f32[4,128,896]{2,1,0:T(8,128)} %fusion.6, f32[4,128,896]{2,1,0:T(8,128)} %fusion.16, f32[4,128]{1,0:T(4,128)S(1)} %copy-done.8, bf16[4,896,128]{2,1,0:T(8,128)(2,1)S(1)} %bitcast.89, pred[896,896]{1,0:T(8,128)(4,1)S(1)} %iota_compare_fusion, ...), kind=kOutput, calls=%fused_computation.18 | convolution fusion | flops 949613056 | bytes 7471104 | tf_op jit(solution)/shard_map/bhts,bshe->bthe/dot_general | solution.py:105
  208.7 0.0 copy-start.9
  208.8 2.0 copy.41
  210.8 0.0 copy-done.9
  210.8 0.5 fusion.3
  211.3 8.3 %convolution_convert_fusion = bf16[3584,2048]{1,0:T(8,128)(2,1)} fusion(bf16[3584,128]{1,0:T(8,128)(2,1)S(1)} %fusion.3, bf16[2048,2048]{1,0:T(8,128)(2,1)} %param.10, s32[]{:T(128)S(6)} %select_n.38), kind=kOutput, calls=%fused_computation | convolution fusion | flops 1886388224 | bytes 16121860 | tf_op jit(solution)/shard_map/dot_general | solution.py:117
  219.7 18.8 %copy.45 = bf16[3584,2048]{0,1:T(8,128)(2,1)} copy(bf16[3584,2048]{1,0:T(8,128)(2,1)} %convolution_convert_fusion) | data formatting | bytes 29360128
  238.5 0.0 reduce-scatter.4.cloned.1.call-update
  238.5 0.0 copy-start.1
  238.5 87.2 %reduce-scatter.4.cloned.1.call-done = bf16[128,3584]{1,0:T(8,128)(2,1)} async-done(((bf16[2048,3584]{1,0:T(8,128)(2,1)}), bf16[128,3584]{1,0:T(8,128)(2,1)}) %reduce-scatter.4.cloned.1.call-update) | async-done | bytes 917520
  325.6 2.2 copy.46
  327.8 0.0 copy-done.1
  (6 shorter events, 0.1 us)
Async XLA Ops:
  6.5 107.9 %copy-start = (bf16[2048,256]{1,0:T(8,128)(2,1)S(1)}, bf16[2048,256]{1,0:T(8,128)(2,1)}, u32[]{:S(2)}) copy-start(bf16[2048,256]{1,0:T(8,128)(2,1)} %param.8) | copy-start | bytes 3145732
  6.5 98.5 %all-gather.5.cloned.1.call-start = ((), (), s32[]{:S(2)}) async-start(), calls=%async_computation.2 | async-start | bytes 15597568 | tf_op jit(solution)/shard_map/all_gather | solution.py:43
  8.5 147.3 %copy-start.5 = (pred[16]{0:T(512)(128)(4,1)}, pred[16]{0:T(512)(128)(4,1)S(1)}, u32[]{:S(2)}) copy-start(pred[16]{0:T(512)(128)(4,1)S(1)} %iota_compare_fusion.1) | copy-start | bytes 52
  147.8 18.4 %copy-start.2 = (f32[4,1,256,128]{3,2,0,1:T(8,128)}, f32[4,1,256,128]{3,2,0,1:T(8,128)S(1)}, u32[]{:S(2)}) copy-start(f32[4,1,256,128]{3,2,0,1:T(8,128)S(1)} %fusion.8) | copy-start | bytes 1572868
  149.0 45.6 %all-to-all-start = ((bf16[16,1,1,256,128]{4,3,2,1,0:T(8,128)(2,1)}), bf16[16,1,1,256,128]{4,3,2,1,0:T(8,128)(2,1)S(1)}, u32[]{:S(2)}, u32[]{:S(2)}) async-start(bf16[16,1,1,256,128]{4,3,2,1,0:T(8,128)(2,1)} %stack.2), calls=%async_computation | async-start | bytes 2097152 | tf_op jit(solution)/shard_map/all_to_all | solution.py:15
  155.0 170.7 %reduce-scatter.4.cloned.1.call-start = ((), (), s32[]{:S(2)}) async-start(), calls=%async_computation.3 | async-start | bytes 15597568
  155.9 9.6 %copy-start.4 = (f32[4,1,128]{2,0,1:T(4,128)S(1)}, f32[4,1,128]{2,0,1:T(4,128)}, u32[]{:S(2)}) copy-start(f32[4,1,128]{2,0,1:T(4,128)} %reduce_window_sum.33) | copy-start | bytes 6148
  155.9 10.2 %copy-start.3 = (bf16[16,128]{1,0:T(8,128)(2,1)S(1)}, bf16[16,128]{1,0:T(8,128)(2,1)}, u32[]{:S(2)}) copy-start(bf16[16,128]{1,0:T(8,128)(2,1)} %get-tuple-element.7) | copy-start | bytes 12292
  155.9 33.5 %copy-start.6 = (pred[16]{0:T(512)(128)(4,1)S(1)}, pred[16]{0:T(512)(128)(4,1)}, u32[]{:S(2)}) copy-start(pred[16]{0:T(512)(128)(4,1)} %copy-done.5) | copy-start | bytes 52
  166.2 28.5 %copy-start.7 = (pred[16]{0:T(512)(128)(4,1)S(1)}, pred[16]{0:T(512)(128)(4,1)}, u32[]{:S(2)}) copy-start(pred[16]{0:T(512)(128)(4,1)} %copy-done.5) | copy-start | bytes 52
  189.5 5.4 %slice-start = ((f32[4,1,256,128]{3,2,0,1:T(8,128)}), f32[3,1,256,128]{3,2,0,1:T(8,128)S(1)}, s32[]{:S(2)}) async-start(f32[4,1,256,128]{3,2,0,1:T(8,128)} %copy-done.2), calls=%async_computation.4 | async-start | bytes 786432 | tf_op jit(solution)/shard_map/slice | solution.py:89
  194.6 5.9 %copy-start.8 = (f32[4,128]{1,0:T(4,128)S(1)}, f32[4,128]{1,0:T(4,128)}, u32[]{:S(2)}) copy-start(f32[4,128]{1,0:T(4,128)} %add_bitcast_fusion) | copy-start | bytes 6148
  208.7 2.1 copy-start.9
  238.5 89.4 %copy-start.1 = (bf16[2048,256]{1,0:T(8,128)(2,1)S(1)}, bf16[2048,256]{1,0:T(8,128)(2,1)}, u32[]{:S(2)}) copy-start(bf16[2048,256]{1,0:T(8,128)(2,1)} %param.8) | copy-start | bytes 3145732
Sparse Core Ops, SparseCore 0:
  9.1 95.8 all-gather.4
  238.6 86.9 reduce-scatter.3
